TPU v7x, 32 devices: a whole 2x2x4 slice. The times are simulated.
32 devices in a mesh: seq: 8 (over y, x, core), batch: 4 (over z).
Axes of the slice: x: 2, y: 2, z: 4, core: 2. Of those that a mesh axis runs over, the one named last changes fastest.
Arguments:
- stream_in: bfloat16 [16, 2048, 768], P('batch', 'seq'), may hold values from -6 to 6
- lengths: int32 [16], P('batch'), may hold values from 64 to 2048, as said below
- token_mask: int32 [16, 2048], P('batch', 'seq'), may hold values from 0 to 1, as said below
- norm1_gain: bfloat16 [768], replicated, may hold values from 0.5 to 1.5
- w_qkv: bfloat16 [768, 2304], replicated, may hold values from -0.21875 to 0.21875
- conv_taps: bfloat16 [3, 2304], replicated, may hold values from -3 to 3
- w_out: bfloat16 [768, 768], replicated, may hold values from -1.75 to 1.75
- norm2_gain: bfloat16 [768], replicated, may hold values from 0.5 to 1.5
- w_up: bfloat16 [768, 3072], replicated, may hold values from -0.21875 to 0.21875
- w_down: bfloat16 [3072, 768], replicated, may hold values from -0.109375 to 0.109375
- grad_output: bfloat16 [16, 2048, 768], P('batch', 'seq'), may hold values from -6 to 6
Outputs:
- stream_out: bfloat16 [16, 2048, 768], P('batch', 'seq')
- grad_input: float32 [16, 2048, 768], P('batch', 'seq')
- grad_norm1: float32 [768], P('batch')
- grad_qkv: float32 [768, 2304], P('batch')
- grad_taps: float32 [3, 2304], replicated
- grad_wout: float32 [768, 768], P('batch')
- grad_norm2: float32 [768], P('batch')
- grad_up: float32 [768, 3072], P('batch')
- grad_down: float32 [3072, 768], P('batch')
- block_rms: float32 [3], replicated
Inputs may be any that keep to these rules, and one draw needn't show every extreme that they name: `lengths`: lengths are heavy tailed over 64 to 2048; some sequence has exactly 2048. `token_mask`: 0 or 1; the first position of every sequence is 1.
All inputs are finite; a program needn't handle non-finite values.
Results may differ from a plain program's by a relative error of at most 0.02.
Values may be sent and summed in bfloat16 or wider, within the bound.
A program may use at most 384 MiB of HBM per device.

v0:
```python
import math
import jax
import jax.numpy as jnp
from jax import lax
from jax.sharding import PartitionSpec as P

HEADS = 12
HEAD = 64


def from_behind(value, axis, steps):
    count = lax.axis_size(axis)
    initial, last = (max(0, -steps), min(count, count - steps))
    return lax.ppermute(value, axis, [(source, source + steps) for source in range(initial, last)])


def dense(left_op, right_op):
    return jnp.dot(left_op, right_op, preferred_element_type=jnp.float32)


def norm_forward(values, gain_vec):
    factor = lax.rsqrt(jnp.mean(values * values, axis=-1, keepdims=True) + 1e-06)
    return (values * factor * gain_vec, factor)


def norm_backward(values, factor, gain_vec, upstream):
    weighted = upstream * gain_vec
    inner_mean = jnp.mean(weighted * values, axis=-1, keepdims=True)
    d_values = factor * weighted - values * (factor * factor * factor) * inner_mean
    d_gain = jnp.sum(upstream * values * factor, axis=(0, 1))
    return (d_values, d_gain)


def split_heads(row_block):
    return row_block.reshape(row_block.shape[0], HEADS, HEAD)


def score_block(q_rows, k_rows, q_begin, k_begin, length):
    factor = 1.0 / math.sqrt(HEAD)
    scores = (
        jnp.einsum(
            "qhe,khe->hqk",
            split_heads(q_rows),
            split_heads(k_rows),
            preferred_element_type=jnp.float32,
        )
        * factor
    )
    q_pos = q_begin + jnp.arange(q_rows.shape[0], dtype=jnp.int32)
    k_pos = k_begin + jnp.arange(k_rows.shape[0], dtype=jnp.int32)
    allowed = (k_pos[None, :] <= q_pos[:, None]) & (k_pos[None, :] < length)
    return (scores, allowed[None])


def attend_forward(q_rows, k_rows, v_rows, length, offset):
    scores, allowed = score_block(q_rows, k_rows, offset, 0, length)
    masked = jnp.where(allowed, scores, -1e30)
    row_max = jnp.max(masked, axis=-1, keepdims=True)
    exp_terms = jnp.exp(masked - row_max)
    row_total = jnp.sum(exp_terms, axis=-1, keepdims=True)
    weights = (exp_terms / row_total).astype(jnp.bfloat16)
    attended = jnp.einsum(
        "hqk,khe->qhe", weights, split_heads(v_rows), preferred_element_type=jnp.float32
    )
    return (attended.reshape(q_rows.shape[0], HEADS * HEAD), (row_max + jnp.log(row_total))[..., 0])


def attend_backward(q_rows, k_rows, v_rows, d_rows, log_total, length, offset):
    scores, allowed = score_block(q_rows, k_rows, offset, 0, length)
    prob_rows = jnp.where(allowed, jnp.exp(scores - log_total[..., None]), 0.0)
    d_probs = jnp.einsum(
        "qhe,khe->hqk", split_heads(d_rows), split_heads(v_rows), preferred_element_type=jnp.float32
    )
    delta_rows = jnp.sum(prob_rows * d_probs, axis=-1, keepdims=True)
    d_scores = (prob_rows * (d_probs - delta_rows)).astype(jnp.bfloat16)
    factor = 1.0 / math.sqrt(HEAD)
    d_query = (
        jnp.einsum(
            "hqk,khe->qhe", d_scores, split_heads(k_rows), preferred_element_type=jnp.float32
        ).reshape(q_rows.shape[0], HEADS * HEAD)
        * factor
    )
    return (d_query, d_scores, prob_rows, delta_rows[..., 0])


def shards(
    stream_in,
    lengths,
    token_mask,
    norm1_gain,
    w_qkv,
    conv_taps,
    w_out,
    norm2_gain,
    w_up,
    w_down,
    grad_output,
):
    seq_count, block_len, model_width = stream_in.shape
    offset = lax.axis_index("seq") * block_len
    factor = 1.0 / math.sqrt(HEAD)
    gain_one = norm1_gain.astype(jnp.float32)
    gain_two = norm2_gain.astype(jnp.float32)
    taps = conv_taps.astype(jnp.float32)
    resid = stream_in.astype(jnp.float32)
    positions = offset + jnp.arange(block_len, dtype=jnp.int32)
    stat_weight = token_mask.astype(jnp.float32) * (positions[None, :] < lengths[:, None]).astype(
        jnp.float32
    )
    cotangent = (grad_output.astype(jnp.float32) * stat_weight[..., None]).astype(jnp.bfloat16)
    normed1, factor_one = norm_forward(resid, gain_one)
    normed1_low = normed1.astype(jnp.bfloat16)
    projected = dense(normed1_low, w_qkv)
    rim_rows = from_behind(projected[:, block_len - 2 :], "seq", 1)
    extended = jnp.concatenate([rim_rows, projected], axis=1)
    mixed = (
        taps[0] * extended[:, 2:]
        + taps[1] * extended[:, 1 : block_len + 1]
        + taps[2] * extended[:, :block_len]
    ).astype(jnp.bfloat16)
    query = mixed[..., :model_width]
    keys_own = mixed[..., model_width : 2 * model_width]
    values_own = mixed[..., 2 * model_width :]
    keys_all, values_all = (
        lax.all_gather(keys_own, "seq", axis=1, tiled=True),
        lax.all_gather(values_own, "seq", axis=1, tiled=True),
    )

    def forward_one(item):
        return attend_forward(item[0], item[1], item[2], item[3], offset)

    attended, log_totals = lax.map(forward_one, (query, keys_all, values_all, lengths))
    attended_low = attended.astype(jnp.bfloat16)
    branch_attn = dense(attended_low, w_out)
    hidden1 = resid + branch_attn
    normed2, factor_two = norm_forward(hidden1, gain_two)
    normed2_low = normed2.astype(jnp.bfloat16)
    up_proj = dense(normed2_low, w_up)
    active = jax.nn.relu(up_proj)
    squared = (active * active).astype(jnp.bfloat16)
    branch_ff = dense(squared, w_down)
    stream_full = hidden1 + branch_ff
    stream_out = stream_full.astype(jnp.bfloat16)

    def masked_square(values):
        return jnp.sum(stat_weight * jnp.sum(values * values, axis=-1))

    local_stats = jnp.stack(
        [
            masked_square(stream_full),
            masked_square(branch_attn),
            masked_square(branch_ff),
            jnp.sum(stat_weight),
        ]
    )
    grad_down = jnp.einsum("scf,scd->fd", squared, cotangent, preferred_element_type=jnp.float32)
    d_squared = jnp.einsum("scd,fd->scf", cotangent, w_down, preferred_element_type=jnp.float32)
    d_up = (2.0 * active * d_squared).astype(jnp.bfloat16)
    grad_up = jnp.einsum("scd,scf->df", normed2_low, d_up, preferred_element_type=jnp.float32)
    d_normed2 = jnp.einsum("scf,df->scd", d_up, w_up, preferred_element_type=jnp.float32)
    d_hidden_norm, grad_norm2 = norm_backward(hidden1, factor_two, gain_two, d_normed2)
    d_hidden1 = cotangent.astype(jnp.float32) + d_hidden_norm
    d_attn = d_hidden1.astype(jnp.bfloat16)
    grad_wout = jnp.einsum("scd,sce->de", attended_low, d_attn, preferred_element_type=jnp.float32)
    d_attended = jnp.einsum(
        "sce,de->scd", d_attn, w_out, preferred_element_type=jnp.float32
    ).astype(jnp.bfloat16)

    def backward_local(item):
        d_query, d_scores, prob_rows, delta_rows = attend_backward(
            item[0], item[1], item[2], item[3], item[4], item[5], offset
        )
        return (d_query, delta_rows)

    d_query_all, delta_all = lax.map(
        backward_local, (query, keys_all, values_all, d_attended, log_totals, lengths)
    )
    lse_rows, delta_rows_all = (
        lax.all_gather(log_totals, "seq", axis=2, tiled=True),
        lax.all_gather(delta_all, "seq", axis=2, tiled=True),
    )
    begin_row = jnp.int32(0)
    q_piece = lax.all_gather(query, "seq", axis=1, tiled=True)
    d_piece = lax.all_gather(d_attended, "seq", axis=1, tiled=True)

    def per_sequence(q_rows, d_rows, k_rows, v_rows, lse_seq, delta_seq, length):
        scores, allowed = score_block(q_rows, k_rows, begin_row, offset, length)
        prob_rows = jnp.where(allowed, jnp.exp(scores - lse_seq[..., None]), 0.0)
        d_probs = jnp.einsum(
            "qhe,khe->hqk",
            split_heads(d_rows),
            split_heads(v_rows),
            preferred_element_type=jnp.float32,
        )
        d_scores = (prob_rows * (d_probs - delta_seq[..., None])).astype(jnp.bfloat16)
        d_keys_part = (
            jnp.einsum(
                "hqk,qhe->khe", d_scores, split_heads(q_rows), preferred_element_type=jnp.float32
            ).reshape(k_rows.shape[0], model_width)
            * factor
        )
        d_values_part = jnp.einsum(
            "hqk,qhe->khe",
            prob_rows.astype(jnp.bfloat16),
            split_heads(d_rows),
            preferred_element_type=jnp.float32,
        ).reshape(k_rows.shape[0], model_width)
        return (d_keys_part, d_values_part)

    d_keys_part, d_values_part = jax.vmap(per_sequence)(
        q_piece, d_piece, keys_own, values_own, lse_rows, delta_rows_all, lengths
    )
    d_mixed = jnp.concatenate([d_query_all, d_keys_part, d_values_part], axis=-1)
    rim_terms = jnp.stack(
        [taps[2] * d_mixed[:, 0], taps[1] * d_mixed[:, 0] + taps[2] * d_mixed[:, 1]], axis=1
    )
    back_rows = from_behind(rim_terms.astype(jnp.bfloat16), "seq", -1).astype(rim_terms.dtype)
    padded = jnp.concatenate(
        [d_mixed, jnp.zeros((seq_count, 2, 3 * model_width), jnp.float32)], axis=1
    )
    d_proj = (
        taps[0] * padded[:, :block_len]
        + taps[1] * padded[:, 1 : block_len + 1]
        + taps[2] * padded[:, 2:]
    )
    d_proj = d_proj + jnp.pad(back_rows, ((0, 0), (block_len - 2, 0), (0, 0)))
    d_proj_low = d_proj.astype(jnp.bfloat16)
    grad_taps = jnp.stack(
        [
            jnp.sum(d_mixed * extended[:, 2:], axis=(0, 1)),
            jnp.sum(d_mixed * extended[:, 1 : block_len + 1], axis=(0, 1)),
            jnp.sum(d_mixed * extended[:, :block_len], axis=(0, 1)),
        ]
    )
    grad_qkv = jnp.einsum(
        "scd,scn->dn", normed1_low, d_proj_low, preferred_element_type=jnp.float32
    )
    d_normed1 = jnp.einsum("scn,dn->scd", d_proj_low, w_qkv, preferred_element_type=jnp.float32)
    d_input_norm, grad_norm1 = norm_backward(resid, factor_one, gain_one, d_normed1)
    grad_input = d_hidden1 + d_input_norm
    shares = (
        lax.psum_scatter(
            grad_norm1.astype(jnp.bfloat16), "batch", scatter_dimension=0, tiled=True
        ).astype(jnp.float32),
        lax.psum_scatter(
            grad_qkv.astype(jnp.bfloat16), "batch", scatter_dimension=0, tiled=True
        ).astype(jnp.float32),
        lax.psum_scatter(
            grad_wout.astype(jnp.bfloat16), "batch", scatter_dimension=0, tiled=True
        ).astype(jnp.float32),
        lax.psum_scatter(
            grad_norm2.astype(jnp.bfloat16), "batch", scatter_dimension=0, tiled=True
        ).astype(jnp.float32),
        lax.psum_scatter(
            grad_up.astype(jnp.bfloat16), "batch", scatter_dimension=0, tiled=True
        ).astype(jnp.float32),
        lax.psum_scatter(
            grad_down.astype(jnp.bfloat16), "batch", scatter_dimension=0, tiled=True
        ).astype(jnp.float32),
    )
    totals = (
        lax.psum(shares[0].astype(jnp.bfloat16), "seq").astype(jnp.float32),
        lax.psum(shares[1].astype(jnp.bfloat16), "seq").astype(jnp.float32),
        lax.psum(shares[2].astype(jnp.bfloat16), "seq").astype(jnp.float32),
        lax.psum(shares[3].astype(jnp.bfloat16), "seq").astype(jnp.float32),
        lax.psum(shares[4].astype(jnp.bfloat16), "seq").astype(jnp.float32),
        lax.psum(shares[5].astype(jnp.bfloat16), "seq").astype(jnp.float32),
    )
    small = lax.psum((grad_taps, local_stats), ("seq", "batch"))
    block_rms = jnp.sqrt(small[1][:3] / (model_width * small[1][3]))
    return (
        stream_out,
        grad_input,
        totals[0],
        totals[1],
        small[0],
        totals[2],
        totals[3],
        totals[4],
        totals[5],
        block_rms,
    )


def solution(mesh):
    return jax.shard_map(
        shards,
        mesh=mesh,
        in_specs=(
            P("batch", "seq", None),
            P("batch"),
            P("batch", "seq"),
            P(),
            P(),
            P(),
            P(),
            P(),
            P(),
            P(),
            P("batch", "seq", None),
        ),
        out_specs=(
            P("batch", "seq", None),
            P("batch", "seq", None),
            P("batch"),
            P("batch", None),
            P(),
            P("batch", None),
            P("batch"),
            P("batch", None),
            P("batch", None),
            P(),
        ),
        check_vma=False,
    )
```

profile of v0, /device:TPU:0, one launch (start us, length us, event | category | flops | bytes accessed | tf_op | source)
XLA Modules:
  0.0 1237.5 jit_solution(3690341579583954142)
XLA Ops:
  23.6 13.4 %constant_dynamic-update-slice_fusion.1 = f32[4,258,2304]{2,0,1:T(4,128)} fusion(f32[4,258,2304]{2,0,1:T(4,128)} %constant_dynamic-update-slice_fusion.2, f32[4,256,2304]{2,1,0:T(8,128)} %copy-done.2), kind=kLoop, calls=%fused_computation.113 | loop fusion | bytes 18874368 | tf_op jit(solution)/shard_map/concatenate | solution.py:115
  37.0 17.5 %add_convert_fusion.1 = bf16[4,256,2304]{2,0,1:T(4,128)(2,1)S(1)} fusion(f32[4,258,2304]{2,0,1:T(4,128)} %constant_dynamic-update-slice_fusion.1, f32[2304]{0:T(1024)S(1)} %get-tuple-element.212, f32[2304]{0:T(1024)} %get-tuple-element.213, f32[2304]{0:T(1024)} %get-tuple-element.211, f32[4,256,2304]{2,1,0:T(8,128)} %copy-done.2), kind=kLoop, calls=%fused_computation.52 | loop fusion | flops 14155776 | bytes 33057792 | tf_op jit(solution)/shard_map/convert_element_type | solution.py:120
  64.8 70.0 %all-gather.7.cloned.1.call-done = bf16[4,2048,768]{2,0,1:T(4,128)(2,1)} async-done(((bf16[4,256,768]{2,0,1:T(4,128)(2,1)}), bf16[4,2048,768]{2,0,1:T(4,128)(2,1)}) %all-gather.7.cloned.1.call-update) | async-done | bytes 12582928 | tf_op jit(solution)/shard_map/all_gather | solution.py:125
  134.8 20.3 %copy.104 = bf16[4,2048,768]{1,2,0:T(8,128)(2,1)} copy(bf16[4,2048,768]{2,0,1:T(4,128)(2,1)} %all-gather.7.cloned.1.call-done) | data formatting | bytes 25165824 | tf_op jit(solution)/shard_map/while | solution.py:132
  155.1 53.8 %all-gather.5.cloned.1.call-done = bf16[4,2048,768]{2,0,1:T(4,128)(2,1)} async-done(((bf16[4,256,768]{2,0,1:T(4,128)(2,1)}), bf16[4,2048,768]{2,0,1:T(4,128)(2,1)}) %all-gather.5.cloned.1.call-update) | async-done | bytes 12582928 | tf_op jit(solution)/shard_map/all_gather | solution.py:126
  208.9 20.3 %copy.102 = bf16[4,2048,768]{1,2,0:T(8,128)(2,1)} copy(bf16[4,2048,768]{2,0,1:T(4,128)(2,1)} %all-gather.5.cloned.1.call-done) | data formatting | bytes 25165824 | tf_op jit(solution)/shard_map/while | solution.py:132
  229.8 170.0 %while.24 = (s32[]{:T(128)}, bf16[4,256,768]{1,2,0:T(8,128)(2,1)}, f32[4,12,256]{2,1,0:T(8,128)}, bf16[4,2048,768]{1,2,0:T(8,128)(2,1)}, s32[]{:T(128)}, /*index...) while((s32[]{:T(128)}, bf16[4,256,768]{1,2,0:T(8,128)(2,1)}, ...), condition=%wide.region_4.5_spmd, body=%wide.region_1.4_spmd.sunk | while | flops 1687158016 | bytes 98936960 | solution.py:132
  236.5 12.3 fusion.108
  260.5 12.0 fusion.110
  474.8 350.4 %while.25 = (s32[]{:T(128)}, f32[4,256,768]{2,0,1:T(4,128)}, f32[4,12,256]{2,1,0:T(8,128)}, bf16[4,2048,768]{1,2,0:T(8,128)(2,1)}, s32[]{:T(128)}, /*index=5*/s3...) while((s32[]{:T(128)}, f32[4,256,768]{2,0,1:T(4,128)}, ...), condition=%wide.region_9.10_spmd, body=%wide.region_7.9_spmd.sunk | while | flops 2486369536 | bytes 169195712 | solution.py:175
  502.7 19.8 %multiply_reduce_fusion.14 = (f32[12,256]{1,0:T(8,128)}, f32[12,256,2048]{2,1,0:T(8,128)}) fusion(f32[12,256,2048]{2,1,0:T(8,128)} %fusion.116, f32[12,256]{1,0:T(8,128)S(1)} %dynamic-slice_bitcast_fusion.2, pred[256,2048]{1,0:T(8,128)(4,1)} %fusion.117, bf16[256,12,64]{0,2,1:T(8,128)(2,1)} %bitcast.149, bf16[2048,12,64]{0,2,1:T(8,128)(2,1)} %bitcast.142), kind=kOutput, calls=%fused_computation.18.clone.1 | convolution fusion | flops 836760576 | bytes 54419456 | tf_op jit(solution)/shard_map/while/body/eval_jaxpr/qhe,khe->hqk/dot_general | solution.py:71
  522.5 20.4 %fusion.118 = f32[12,64,256]{2,1,0:T(8,128)} fusion(bf16[2048,12,64]{0,2,1:T(8,128)(2,1)} %bitcast.140, f32[12,256,2048]{2,1,0:T(8,128)} %get-tuple-element.413, f32[12,256,2048]{2,1,0:T(8,128)} %fusion.116, f32[12,256]{1,0:T(8,128)} %get-tuple-element.414, f32[12,256]{1,0:T(8,128)S(1)} %dynamic-slice_bitcast_fusion.2, pred[256,2048]{1,0:T(8,128)(4,1)} %fusion.117), kind=kOutput, calls=%fused_computation.24.clone.1 | convolution fusion | flops 843251712 | bytes 54812672 | tf_op jit(solution)/shard_map/while/body/eval_jaxpr/hqk,khe->qhe/dot_general | solution.py:78
  547.3 15.6 %dynamic_update_slice.24 = f32[4,256,768]{2,0,1:T(4,128)} dynamic-update-slice(f32[4,256,768]{2,0,1:T(4,128)} %get-tuple-element.455, f32[1,256,768]{2,0,1:T(1,128)} %copy.160, s32[]{:T(128)S(6)} %copy.178, s32[]{:T(128)} %constant.66.clone.1..sunk, s32[]{:T(128)} %constant.66.clone.1..sunk) | dynamic-update-slice | bytes 1572868 | tf_op jit(solution)/shard_map/while/body/jit(dynamic_update_index_in_dim)/dynamic_update_slice | solution.py:132
  590.6 19.8 %multiply_reduce_fusion.14 = (f32[12,256]{1,0:T(8,128)}, f32[12,256,2048]{2,1,0:T(8,128)}) fusion(f32[12,256,2048]{2,1,0:T(8,128)} %fusion.116, f32[12,256]{1,0:T(8,128)S(1)} %dynamic-slice_bitcast_fusion.2, pred[256,2048]{1,0:T(8,128)(4,1)} %fusion.117, bf16[256,12,64]{0,2,1:T(8,128)(2,1)} %bitcast.149, bf16[2048,12,64]{0,2,1:T(8,128)(2,1)} %bitcast.142), kind=kOutput, calls=%fused_computation.18.clone.1 | convolution fusion | flops 836760576 | bytes 54419456 | tf_op jit(solution)/shard_map/while/body/eval_jaxpr/qhe,khe->hqk/dot_general | solution.py:71
  610.4 20.3 %fusion.118 = f32[12,64,256]{2,1,0:T(8,128)} fusion(bf16[2048,12,64]{0,2,1:T(8,128)(2,1)} %bitcast.140, f32[12,256,2048]{2,1,0:T(8,128)} %get-tuple-element.413, f32[12,256,2048]{2,1,0:T(8,128)} %fusion.116, f32[12,256]{1,0:T(8,128)} %get-tuple-element.414, f32[12,256]{1,0:T(8,128)S(1)} %dynamic-slice_bitcast_fusion.2, pred[256,2048]{1,0:T(8,128)(4,1)} %fusion.117), kind=kOutput, calls=%fused_computation.24.clone.1 | convolution fusion | flops 843251712 | bytes 54812672 | tf_op jit(solution)/shard_map/while/body/eval_jaxpr/hqk,khe->qhe/dot_general | solution.py:78
  635.1 15.5 %dynamic_update_slice.24 = f32[4,256,768]{2,0,1:T(4,128)} dynamic-update-slice(f32[4,256,768]{2,0,1:T(4,128)} %get-tuple-element.455, f32[1,256,768]{2,0,1:T(1,128)} %copy.160, s32[]{:T(128)S(6)} %copy.178, s32[]{:T(128)} %constant.66.clone.1..sunk, s32[]{:T(128)} %constant.66.clone.1..sunk) | dynamic-update-slice | bytes 1572868 | tf_op jit(solution)/shard_map/while/body/jit(dynamic_update_index_in_dim)/dynamic_update_slice | solution.py:132
  678.2 19.8 %multiply_reduce_fusion.14 = (f32[12,256]{1,0:T(8,128)}, f32[12,256,2048]{2,1,0:T(8,128)}) fusion(f32[12,256,2048]{2,1,0:T(8,128)} %fusion.116, f32[12,256]{1,0:T(8,128)S(1)} %dynamic-slice_bitcast_fusion.2, pred[256,2048]{1,0:T(8,128)(4,1)} %fusion.117, bf16[256,12,64]{0,2,1:T(8,128)(2,1)} %bitcast.149, bf16[2048,12,64]{0,2,1:T(8,128)(2,1)} %bitcast.142), kind=kOutput, calls=%fused_computation.18.clone.1 | convolution fusion | flops 836760576 | bytes 54419456 | tf_op jit(solution)/shard_map/while/body/eval_jaxpr/qhe,khe->hqk/dot_general | solution.py:71
  697.9 20.1 %fusion.118 = f32[12,64,256]{2,1,0:T(8,128)} fusion(bf16[2048,12,64]{0,2,1:T(8,128)(2,1)} %bitcast.140, f32[12,256,2048]{2,1,0:T(8,128)} %get-tuple-element.413, f32[12,256,2048]{2,1,0:T(8,128)} %fusion.116, f32[12,256]{1,0:T(8,128)} %get-tuple-element.414, f32[12,256]{1,0:T(8,128)S(1)} %dynamic-slice_bitcast_fusion.2, pred[256,2048]{1,0:T(8,128)(4,1)} %fusion.117), kind=kOutput, calls=%fused_computation.24.clone.1 | convolution fusion | flops 843251712 | bytes 54812672 | tf_op jit(solution)/shard_map/while/body/eval_jaxpr/hqk,khe->qhe/dot_general | solution.py:78
  722.4 15.5 %dynamic_update_slice.24 = f32[4,256,768]{2,0,1:T(4,128)} dynamic-update-slice(f32[4,256,768]{2,0,1:T(4,128)} %get-tuple-element.455, f32[1,256,768]{2,0,1:T(1,128)} %copy.160, s32[]{:T(128)S(6)} %copy.178, s32[]{:T(128)} %constant.66.clone.1..sunk, s32[]{:T(128)} %constant.66.clone.1..sunk) | dynamic-update-slice | bytes 1572868 | tf_op jit(solution)/shard_map/while/body/jit(dynamic_update_index_in_dim)/dynamic_update_slice | solution.py:132
  765.5 19.8 %multiply_reduce_fusion.14 = (f32[12,256]{1,0:T(8,128)}, f32[12,256,2048]{2,1,0:T(8,128)}) fusion(f32[12,256,2048]{2,1,0:T(8,128)} %fusion.116, f32[12,256]{1,0:T(8,128)S(1)} %dynamic-slice_bitcast_fusion.2, pred[256,2048]{1,0:T(8,128)(4,1)} %fusion.117, bf16[256,12,64]{0,2,1:T(8,128)(2,1)} %bitcast.149, bf16[2048,12,64]{0,2,1:T(8,128)(2,1)} %bitcast.142), kind=kOutput, calls=%fused_computation.18.clone.1 | convolution fusion | flops 836760576 | bytes 54419456 | tf_op jit(solution)/shard_map/while/body/eval_jaxpr/qhe,khe->hqk/dot_general | solution.py:71
  785.2 20.1 %fusion.118 = f32[12,64,256]{2,1,0:T(8,128)} fusion(bf16[2048,12,64]{0,2,1:T(8,128)(2,1)} %bitcast.140, f32[12,256,2048]{2,1,0:T(8,128)} %get-tuple-element.413, f32[12,256,2048]{2,1,0:T(8,128)} %fusion.116, f32[12,256]{1,0:T(8,128)} %get-tuple-element.414, f32[12,256]{1,0:T(8,128)S(1)} %dynamic-slice_bitcast_fusion.2, pred[256,2048]{1,0:T(8,128)(4,1)} %fusion.117), kind=kOutput, calls=%fused_computation.24.clone.1 | convolution fusion | flops 843251712 | bytes 54812672 | tf_op jit(solution)/shard_map/while/body/eval_jaxpr/hqk,khe->qhe/dot_general | solution.py:78
  809.7 15.5 %dynamic_update_slice.24 = f32[4,256,768]{2,0,1:T(4,128)} dynamic-update-slice(f32[4,256,768]{2,0,1:T(4,128)} %get-tuple-element.455, f32[1,256,768]{2,0,1:T(1,128)} %copy.160, s32[]{:T(128)S(6)} %copy.178, s32[]{:T(128)} %constant.66.clone.1..sunk, s32[]{:T(128)} %constant.66.clone.1..sunk) | dynamic-update-slice | bytes 1572868 | tf_op jit(solution)/shard_map/while/body/jit(dynamic_update_index_in_dim)/dynamic_update_slice | solution.py:132
  857.3 20.1 %copy.110 = bf16[4,2048,768]{1,2,0:T(8,128)(2,1)} copy(bf16[4,2048,768]{2,0,1:T(4,128)(2,1)} %all-gather.9.cloned.1.call-done) | data formatting | bytes 25165824 | tf_op jit(solution)/shard_map/all_gather | solution.py:183
  877.5 39.7 %fusion.62 = f32[4,12,2048,256]{3,2,1,0:T(8,128)} fusion(bf16[4,2048,12,64]{1,3,2,0:T(8,128)(2,1)} %bitcast.147, bf16[4,256,12,64]{1,3,2,0:T(8,128)(2,1)} %bitcast.153), kind=kOutput, calls=%fused_computation.137 | convolution fusion | flops 3221225472 | bytes 114819072 | tf_op jit(solution)/shard_map/vmap(qhe,khe->hqk)/dot_general | solution.py:41
  917.2 16.0 %copy.112 = bf16[4,2048,768]{1,2,0:T(8,128)(2,1)} copy(bf16[4,2048,768]{2,1,0:T(8,128)(2,1)} %all-gather.11.cloned.1.call-done) | data formatting | bytes 25165824 | tf_op jit(solution)/shard_map/all_gather | solution.py:184
  933.2 38.9 %fusion.13 = f32[4,12,64,256]{3,2,1,0:T(8,128)} fusion(bf16[4,2048,12,64]{1,3,2,0:T(8,128)(2,1)} %bitcast.150, f32[4,12,2048,256]{3,2,1,0:T(8,128)} %fusion.62, f32[4,12,2048]{2,1,0:T(8,128)} %all_gather.21, pred[4,2048,256]{2,1,0:T(8,128)(4,1)} %broadcast_and_fusion), kind=kOutput, calls=%fused_computation.38 | convolution fusion | flops 3321888768 | bytes 118882304 | tf_op jit(solution)/shard_map/vmap(hqk,qhe->khe)/dot_general | solution.py:202
  977.1 51.0 %fusion.42 = f32[4,12,64,256]{3,2,1,0:T(8,128)} fusion(bf16[4,2048,12,64]{1,3,2,0:T(8,128)(2,1)} %bitcast.148, f32[4,12,2048,256]{3,2,1,0:T(8,128)} %fusion.62, f32[4,12,2048]{2,1,0:T(8,128)} %all_gather.23, f32[4,12,2048]{2,1,0:T(8,128)} %all_gather.21, pred[4,2048,256]{2,1,0:T(8,128)(4,1)} %broadcast_and_fusion, bf16[4,2048,12,64]{1,3,2,0:T(8,128)(2,1)} %bitcast.151, ...), kind=kOutput, calls=%fused_computation.94 | convolution fusion | flops 6594232320 | bytes 133431296 | tf_op jit(solution)/shard_map/vmap(hqk,qhe->khe)/dot_general | solution.py:197
  1033.0 20.5 %multiply_reduce_fusion.2 = (f32[2304]{0:T(1024)}, f32[2304]{0:T(1024)}, f32[2304]{0:T(1024)S(1)}, f32[4,256,2304]{2,0,1:T(4,128)S(1)}) fusion(f32[4,258,2304]{2,0,1:T(4,128)} %constant_dynamic-update-slice_fusion.1, f32[4,256,768]{2,0,1:T(4,128)} %copy.116, f32[4,256,768]{2,0,1:T(4,128)} %copy.115, f32[4,256,768]{2,0,1:T(4,128)} %get-tuple-element.108, ...), kind=kLoop, calls=%fused_computation.49 | loop fusion | flops 18867456 | bytes 47213568 | tf_op jit(solution)/shard_map/reduce_sum | solution.py:231
  1082.8 47.2 %all-reduce.4 = (f32[3,2304]{1,0:T(4,128)}, f32[4]{0:T(128)S(1)}) all-reduce(f32[3,2304]{1,0:T(4,128)} %pad_maximum_fusion.2, f32[4]{0:T(128)} %pad_maximum_fusion.3), channel_id=1, replica_groups=mesh['seq'=8,'batch'=4] {'seq','batch'}, use_global_device_ids=true, to_apply=%region_19.20 | all-reduce | flops 6916 | bytes 55328 | tf_op jit(solution)/shard_map/psum | solution.py:269
  1131.3 13.2 %reduce-scatter.5.cloned.1.call-done = bf16[192,2304]{1,0:T(8,128)(2,1)} async-done(((bf16[768,2304]{1,0:T(8,128)(2,1)}), bf16[192,2304]{1,0:T(8,128)(2,1)}) %reduce-scatter.5.cloned.1.call-update) | async-done | bytes 884752 | tf_op jit(solution)/shard_map/reduce_scatter | solution.py:245
  1167.7 12.5 %all-reduce.5 = (bf16[192]{0:T(256)(128)(2,1)}, bf16[192]{0:T(256)(128)(2,1)}) all-reduce(bf16[192]{0:T(256)(128)(2,1)S(1)} %dynamic-slice.1, bf16[192]{0:T(256)(128)(2,1)} %dynamic-slice.3), channel_id=1, replica_groups=mesh['seq'=8,'batch'=4] {'seq'}, use_global_device_ids=true, to_apply=%region_13.14 | all-reduce | flops 384 | bytes 1536 | tf_op jit(solution)/shard_map/psum | solution.py:262
  1188.3 34.7 %all-reduce.10.cloned.1.call-done = (bf16[192,2304]{1,0:T(8,128)(2,1)}, bf16[192,768]{1,0:T(8,128)(2,1)}, bf16[192,3072]{1,0:T(8,128)(2,1)}, bf16[768,768]{1,0:T(8,128)(2,1)}) async-done(((bf16[192,2304]{1,0:T(8,128)(2,1)}, bf16[192,768]{1,0:T(8,128)(2,1)}, bf16[192,3072]{1,0:T(8,128)(2,1)}, bf16[768,768]{1,0:T(8,128)(2,1)}), (bf16[192,2304]{1,0:T(8,128)(2,1)}, bf16[192,768]{1,0:T(8,128)(2,1)}, ...) | async-done | bytes 3538960 | tf_op jit(solution)/shard_map/psum | solution.py:263
  (259 shorter events, 485.8 us)
Async XLA Ops:
  7.2 127.6 %all-gather.7.cloned.1.call-start = ((), (), s32[]{:S(2)}) async-start(), calls=%async_computation.5 | async-start | bytes 14155776 | tf_op jit(solution)/shard_map/all_gather | solution.py:125
  8.1 8.0 copy-start.23
  10.7 5.4 copy-start.20
  10.7 11.6 copy-start.16
  19.7 3.3 collective-permute-start
  22.9 14.0 %copy-start.10 = (f32[2304]{0:T(1024)}, f32[2304]{0:T(1024)S(1)}, u32[]{:S(2)}) copy-start(f32[2304]{0:T(1024)S(1)} %get-tuple-element.212) | copy-start | bytes 27652
  57.4 151.4 %all-gather.5.cloned.1.call-start = ((), (), s32[]{:S(2)}) async-start(), calls=%async_computation.4 | async-start | bytes 14155776 | tf_op jit(solution)/shard_map/all_gather | solution.py:126
  58.2 799.2 %all-gather.9.cloned.1.call-start = ((), (), s32[]{:S(2)}) async-start(), calls=%async_computation.6 | async-start | bytes 14155776 | tf_op jit(solution)/shard_map/all_gather | solution.py:183
  64.5 852.7 %all-gather.11.cloned.1.call-start = ((), (), s32[]{:S(2)}) async-start(), calls=%async_computation.7 | async-start | bytes 14155776 | tf_op jit(solution)/shard_map/all_gather | solution.py:184
  399.8 13.6 %slice-start = ((s8[4718592]{0:T(1024)(128)(4,1)}), s8[4194304]{0:T(1024)(128)(4,1)S(1)}, s32[]{:S(2)}) async-start(s8[4718592]{0:T(1024)(128)(4,1)} %bitcast.157), calls=%async_computation.13 | async-start | bytes 8388608
  404.9 36.1 %copy-start.6 = (f32[4,256,768]{2,1,0:T(8,128)}, f32[4,256,768]{2,1,0:T(8,128)S(1)}, u32[]{:S(2)}) copy-start(f32[4,256,768]{2,1,0:T(8,128)S(1)} %get-tuple-element.267) | copy-start | bytes 9437188
  404.9 36.1 %copy-start.17 = (f32[4,256]{1,0:T(4,128)}, f32[4,256]{1,0:T(4,128)S(1)}, u32[]{:S(2)}) copy-start(f32[4,256]{1,0:T(4,128)S(1)} %get-tuple-element.287) | copy-start | bytes 12292
  404.9 8.5 copy-start.7
  404.9 8.5 copy-start.14
  404.9 8.5 slice-start.1
  446.4 684.8 %reduce-scatter.7.cloned.1.call-start = ((), (), s32[]{:S(2)}) async-start(), calls=%async_computation.9 | async-start | bytes 1474560 | tf_op jit(solution)/shard_map/reduce_scatter | solution.py:248
  452.5 678.8 %reduce-scatter.11.cloned.1.call-start = ((), (), s32[]{:S(2)}) async-start(), calls=%async_computation.11 | async-start | bytes 5898240 | tf_op jit(solution)/shard_map/reduce_scatter | solution.py:257
  474.1 657.1 %reduce-scatter.9.cloned.1.call-start = ((), (), s32[]{:S(2)}) async-start(), calls=%async_computation.10 | async-start | bytes 5898240 | tf_op jit(solution)/shard_map/reduce_scatter | solution.py:254
  857.3 287.2 %reduce-scatter.5.cloned.1.call-start = ((), (), s32[]{:S(2)}) async-start(), calls=%async_computation.8 | async-start | bytes 4423680 | tf_op jit(solution)/shard_map/reduce_scatter | solution.py:245
  1033.0 20.5 %copy-start.11 = (f32[2304]{0:T(1024)S(1)}, f32[2304]{0:T(1024)}, u32[]{:S(2)}) copy-start(f32[2304]{0:T(1024)} %copy-done.10) | copy-start | bytes 27652
  1033.0 20.5 %copy-start.12 = (f32[2304]{0:T(1024)S(1)}, f32[2304]{0:T(1024)}, u32[]{:S(2)}) copy-start(f32[2304]{0:T(1024)} %get-tuple-element.213) | copy-start | bytes 27652
  1033.0 24.4 %copy-start.13 = (f32[2304]{0:T(1024)S(1)}, f32[2304]{0:T(1024)}, u32[]{:S(2)}) copy-start(f32[2304]{0:T(1024)} %get-tuple-element.211) | copy-start | bytes 27652
  1053.6 15.0 %copy-start.4 = (bf16[4,256,768]{2,1,0:T(8,128)(2,1)S(1)}, bf16[4,256,768]{2,1,0:T(8,128)(2,1)}, u32[]{:S(2)}) copy-start(bf16[4,256,768]{2,1,0:T(8,128)(2,1)} %param.15) | copy-start | bytes 4718596
  1053.6 15.0 %copy-start.21 = (f32[4,256]{1,0:T(4,128)S(1)}, f32[4,256]{1,0:T(4,128)}, u32[]{:S(2)}) copy-start(f32[4,256]{1,0:T(4,128)} %copy-done.20) | copy-start | bytes 12292
  1053.6 15.0 %copy-start.24 = (f32[768]{0:T(1024)S(1)}, f32[768]{0:T(1024)}, u32[]{:S(2)}) copy-start(f32[768]{0:T(1024)} %copy-done.23) | copy-start | bytes 9220
  1053.7 3.8 collective-permute-start.1
  1074.2 148.8 %all-reduce.10.cloned.1.call-start = ((), (), s32[]{:S(2)}) async-start(), calls=%async_computation.12 | async-start | bytes 7077888 | tf_op jit(solution)/shard_map/psum | solution.py:263
  1077.5 67.5 %copy-start.22 = (f32[4,256]{1,0:T(4,128)S(1)}, f32[4,256]{1,0:T(4,128)}, u32[]{:S(2)}) copy-start(f32[4,256]{1,0:T(4,128)} %copy-done.20) | copy-start | bytes 12292
  1082.1 62.9 %copy-start.25 = (f32[768]{0:T(1024)S(1)}, f32[768]{0:T(1024)}, u32[]{:S(2)}) copy-start(f32[768]{0:T(1024)} %copy-done.23) | copy-start | bytes 9220
  1145.0 9.2 copy-start.31
  1145.0 38.4 %copy-start.19 = (f32[4,256]{1,0:T(4,128)S(1)}, f32[4,256]{1,0:T(4,128)}, u32[]{:S(2)}) copy-start(f32[4,256]{1,0:T(4,128)} %get-tuple-element.284) | copy-start | bytes 12292
  1223.0 6.1 copy-start.8
  (18 other events, 54.3 us)
Sparse Core Ops, SparseCore 0:
  57.5 77.2 all-gather.6
  136.7 72.1 all-gather.4
  210.8 72.1 all-gather.8
  446.5 72.1 all-gather.10
  520.9 29.1 reduce-scatter.6
  552.3 83.9 reduce-scatter.10
  857.4 85.4 reduce-scatter.8
  1074.3 70.0 reduce-scatter.4
  1148.1 74.8 all-reduce.9
where the time goes:
time: 1250 us; the launch traced here: 1240 us
  matrix products  510 us (41%)
  local copies, waits for them, and re-layouts  291 us (23%)
  waiting for transfers between devices  175 us (14%)
  other arithmetic  147 us (12%)
  blocking collectives  93.4 us (7%)
  between operations  15.8 us (1%)
    dot_general x9, matrix products, score_block(): jnp.einsum('qhe,khe->hqk', split_heads(q_rows), split_heads(k_rows), pref...  124 us
    dynamic_update_slice x16, local copies, waits for them, and re-layouts, shards(): lax.map(forward_one, (query, keys_all, values_all, lengths))  82.7 us
    dot_general x4, matrix products, attend_backward(): jnp.einsum('hqk,khe->qhe', d_scores, split_heads(k_rows), preferred_eleme...  81 us
    dot_general x4, matrix products, attend_backward(): jnp.einsum('qhe,khe->hqk', split_heads(d_rows), split_heads(v_rows), pref...  79.1 us
    all_gather x1, waiting for transfers between devices, shards(): lax.all_gather(keys_own, 'seq', axis=1, tiled=True)  70 us
    dynamic_slice x32, local copies, waits for them, and re-layouts, shards(): lax.map(forward_one, (query, keys_all, values_all, lengths))  68.3 us
    all_gather x1, waiting for transfers between devices, shards(): lax.all_gather(values_own, 'seq', axis=1, tiled=True)  53.8 us
    dot_general x1, matrix products, per_sequence(): jnp.einsum('hqk,qhe->khe', d_scores, split_heads(q_rows), preferred_eleme...  51 us
  transfers between devices with their start and end apart: 11, of which 5 were waited for; matrix products, arithmetic and copies ran while one was open for 71% of the time, Pallas kernels for 0%

commit v1 on v0

--- a/solution.py
+++ b/solution.py
@@ -266,7 +266,9 @@
         lax.psum(shares[4].astype(jnp.bfloat16), "seq").astype(jnp.float32),
         lax.psum(shares[5].astype(jnp.bfloat16), "seq").astype(jnp.float32),
     )
-    small = lax.psum((grad_taps, local_stats), ("seq", "batch"))
+    small = (grad_taps, local_stats)
+    for name in ("seq", "batch"):
+        small = lax.psum(small, name)
     block_rms = jnp.sqrt(small[1][:3] / (model_width * small[1][3]))
     return (
         stream_out,

time: 1250 us -> 1250 us (level)
    psum x1 -> x2, blocking collectives: 47.2 us -> 52.1 us  [shards(): small = lax.psum(small, name)]
where the time goes in v1:
time: 1250 us; the launch traced here: 1240 us
  matrix products  510 us (41%)
  local copies, waits for them, and re-layouts  291 us (23%)
  waiting for transfers between devices  171 us (14%)
  other arithmetic  147 us (12%)
  blocking collectives  98.1 us (8%)
  between operations  15.8 us (1%)
    dot_general x9, matrix products, score_block(): jnp.einsum('qhe,khe->hqk', split_heads(q_rows), split_heads(k_rows), pref...  124 us
    dynamic_update_slice x16, local copies, waits for them, and re-layouts, shards(): lax.map(forward_one, (query, keys_all, values_all, lengths))  82.7 us
    dot_general x4, matrix products, attend_backward(): jnp.einsum('hqk,khe->qhe', d_scores, split_heads(k_rows), preferred_eleme...  81 us
    dot_general x4, matrix products, attend_backward(): jnp.einsum('qhe,khe->hqk', split_heads(d_rows), split_heads(v_rows), pref...  79.1 us
    all_gather x1, waiting for transfers between devices, shards(): lax.all_gather(keys_own, 'seq', axis=1, tiled=True)  70 us
    dynamic_slice x32, local copies, waits for them, and re-layouts, shards(): lax.map(forward_one, (query, keys_all, values_all, lengths))  68.3 us
    all_gather x1, waiting for transfers between devices, shards(): lax.all_gather(values_own, 'seq', axis=1, tiled=True)  53.8 us
    psum x2, blocking collectives, shards(): small = lax.psum(small, name)  52.1 us
  transfers between devices with their start and end apart: 11, of which 5 were waited for; matrix products, arithmetic and copies ran while one was open for 71% of the time, Pallas kernels for 0%

profile of v1, /device:TPU:0, one launch (start us, length us, event | category | flops | bytes accessed | tf_op | source)
XLA Modules:
  0.0 1237.9 jit_solution(437977196219980184)
XLA Ops:
  23.6 13.4 %constant_dynamic-update-slice_fusion.1 = f32[4,258,2304]{2,0,1:T(4,128)} fusion(f32[4,258,2304]{2,0,1:T(4,128)} %constant_dynamic-update-slice_fusion.2, f32[4,256,2304]{2,1,0:T(8,128)} %copy-done.2), kind=kLoop, calls=%fused_computation.113 | loop fusion | bytes 18874368 | tf_op jit(solution)/shard_map/concatenate | solution.py:115
  37.0 17.5 %add_convert_fusion.1 = bf16[4,256,2304]{2,0,1:T(4,128)(2,1)S(1)} fusion(f32[4,258,2304]{2,0,1:T(4,128)} %constant_dynamic-update-slice_fusion.1, f32[2304]{0:T(1024)S(1)} %get-tuple-element.212, f32[2304]{0:T(1024)} %get-tuple-element.213, f32[2304]{0:T(1024)} %get-tuple-element.211, f32[4,256,2304]{2,1,0:T(8,128)} %copy-done.2), kind=kLoop, calls=%fused_computation.52 | loop fusion | flops 14155776 | bytes 33057792 | tf_op jit(solution)/shard_map/convert_element_type | solution.py:120
  64.8 70.0 %all-gather.7.cloned.1.call-done = bf16[4,2048,768]{2,0,1:T(4,128)(2,1)} async-done(((bf16[4,256,768]{2,0,1:T(4,128)(2,1)}), bf16[4,2048,768]{2,0,1:T(4,128)(2,1)}) %all-gather.7.cloned.1.call-update) | async-done | bytes 12582928 | tf_op jit(solution)/shard_map/all_gather | solution.py:125
  134.8 20.3 %copy.104 = bf16[4,2048,768]{1,2,0:T(8,128)(2,1)} copy(bf16[4,2048,768]{2,0,1:T(4,128)(2,1)} %all-gather.7.cloned.1.call-done) | data formatting | bytes 25165824 | tf_op jit(solution)/shard_map/while | solution.py:132
  155.1 53.8 %all-gather.5.cloned.1.call-done = bf16[4,2048,768]{2,0,1:T(4,128)(2,1)} async-done(((bf16[4,256,768]{2,0,1:T(4,128)(2,1)}), bf16[4,2048,768]{2,0,1:T(4,128)(2,1)}) %all-gather.5.cloned.1.call-update) | async-done | bytes 12582928 | tf_op jit(solution)/shard_map/all_gather | solution.py:126
  208.9 20.3 %copy.102 = bf16[4,2048,768]{1,2,0:T(8,128)(2,1)} copy(bf16[4,2048,768]{2,0,1:T(4,128)(2,1)} %all-gather.5.cloned.1.call-done) | data formatting | bytes 25165824 | tf_op jit(solution)/shard_map/while | solution.py:132
  229.8 170.0 %while.24 = (s32[]{:T(128)}, bf16[4,256,768]{1,2,0:T(8,128)(2,1)}, f32[4,12,256]{2,1,0:T(8,128)}, bf16[4,2048,768]{1,2,0:T(8,128)(2,1)}, s32[]{:T(128)}, /*index...) while((s32[]{:T(128)}, bf16[4,256,768]{1,2,0:T(8,128)(2,1)}, ...), condition=%wide.region_4.5_spmd, body=%wide.region_1.4_spmd.sunk | while | flops 1687158016 | bytes 98936960 | solution.py:132
  236.5 12.3 fusion.108
  260.5 12.0 fusion.110
  474.8 350.4 %while.25 = (s32[]{:T(128)}, f32[4,256,768]{2,0,1:T(4,128)}, f32[4,12,256]{2,1,0:T(8,128)}, bf16[4,2048,768]{1,2,0:T(8,128)(2,1)}, s32[]{:T(128)}, /*index=5*/s3...) while((s32[]{:T(128)}, f32[4,256,768]{2,0,1:T(4,128)}, ...), condition=%wide.region_9.10_spmd, body=%wide.region_7.9_spmd.sunk | while | flops 2486369536 | bytes 169195712 | solution.py:175
  502.7 19.8 %multiply_reduce_fusion.14 = (f32[12,256]{1,0:T(8,128)}, f32[12,256,2048]{2,1,0:T(8,128)}) fusion(f32[12,256,2048]{2,1,0:T(8,128)} %fusion.116, f32[12,256]{1,0:T(8,128)S(1)} %dynamic-slice_bitcast_fusion.2, pred[256,2048]{1,0:T(8,128)(4,1)} %fusion.117, bf16[256,12,64]{0,2,1:T(8,128)(2,1)} %bitcast.149, bf16[2048,12,64]{0,2,1:T(8,128)(2,1)} %bitcast.142), kind=kOutput, calls=%fused_computation.18.clone.1 | convolution fusion | flops 836760576 | bytes 54419456 | tf_op jit(solution)/shard_map/while/body/eval_jaxpr/qhe,khe->hqk/dot_general | solution.py:71
  522.5 20.4 %fusion.118 = f32[12,64,256]{2,1,0:T(8,128)} fusion(bf16[2048,12,64]{0,2,1:T(8,128)(2,1)} %bitcast.140, f32[12,256,2048]{2,1,0:T(8,128)} %get-tuple-element.415, f32[12,256,2048]{2,1,0:T(8,128)} %fusion.116, f32[12,256]{1,0:T(8,128)} %get-tuple-element.416, f32[12,256]{1,0:T(8,128)S(1)} %dynamic-slice_bitcast_fusion.2, pred[256,2048]{1,0:T(8,128)(4,1)} %fusion.117), kind=kOutput, calls=%fused_computation.24.clone.1 | convolution fusion | flops 843251712 | bytes 54812672 | tf_op jit(solution)/shard_map/while/body/eval_jaxpr/hqk,khe->qhe/dot_general | solution.py:78
  547.3 15.6 %dynamic_update_slice.24 = f32[4,256,768]{2,0,1:T(4,128)} dynamic-update-slice(f32[4,256,768]{2,0,1:T(4,128)} %get-tuple-element.457, f32[1,256,768]{2,0,1:T(1,128)} %copy.160, s32[]{:T(128)S(6)} %copy.178, s32[]{:T(128)} %constant.66.clone.1..sunk, s32[]{:T(128)} %constant.66.clone.1..sunk) | dynamic-update-slice | bytes 1572868 | tf_op jit(solution)/shard_map/while/body/jit(dynamic_update_index_in_dim)/dynamic_update_slice | solution.py:132
  590.6 19.8 %multiply_reduce_fusion.14 = (f32[12,256]{1,0:T(8,128)}, f32[12,256,2048]{2,1,0:T(8,128)}) fusion(f32[12,256,2048]{2,1,0:T(8,128)} %fusion.116, f32[12,256]{1,0:T(8,128)S(1)} %dynamic-slice_bitcast_fusion.2, pred[256,2048]{1,0:T(8,128)(4,1)} %fusion.117, bf16[256,12,64]{0,2,1:T(8,128)(2,1)} %bitcast.149, bf16[2048,12,64]{0,2,1:T(8,128)(2,1)} %bitcast.142), kind=kOutput, calls=%fused_computation.18.clone.1 | convolution fusion | flops 836760576 | bytes 54419456 | tf_op jit(solution)/shard_map/while/body/eval_jaxpr/qhe,khe->hqk/dot_general | solution.py:71
  610.4 20.3 %fusion.118 = f32[12,64,256]{2,1,0:T(8,128)} fusion(bf16[2048,12,64]{0,2,1:T(8,128)(2,1)} %bitcast.140, f32[12,256,2048]{2,1,0:T(8,128)} %get-tuple-element.415, f32[12,256,2048]{2,1,0:T(8,128)} %fusion.116, f32[12,256]{1,0:T(8,128)} %get-tuple-element.416, f32[12,256]{1,0:T(8,128)S(1)} %dynamic-slice_bitcast_fusion.2, pred[256,2048]{1,0:T(8,128)(4,1)} %fusion.117), kind=kOutput, calls=%fused_computation.24.clone.1 | convolution fusion | flops 843251712 | bytes 54812672 | tf_op jit(solution)/shard_map/while/body/eval_jaxpr/hqk,khe->qhe/dot_general | solution.py:78
  635.1 15.5 %dynamic_update_slice.24 = f32[4,256,768]{2,0,1:T(4,128)} dynamic-update-slice(f32[4,256,768]{2,0,1:T(4,128)} %get-tuple-element.457, f32[1,256,768]{2,0,1:T(1,128)} %copy.160, s32[]{:T(128)S(6)} %copy.178, s32[]{:T(128)} %constant.66.clone.1..sunk, s32[]{:T(128)} %constant.66.clone.1..sunk) | dynamic-update-slice | bytes 1572868 | tf_op jit(solution)/shard_map/while/body/jit(dynamic_update_index_in_dim)/dynamic_update_slice | solution.py:132
  678.2 19.8 %multiply_reduce_fusion.14 = (f32[12,256]{1,0:T(8,128)}, f32[12,256,2048]{2,1,0:T(8,128)}) fusion(f32[12,256,2048]{2,1,0:T(8,128)} %fusion.116, f32[12,256]{1,0:T(8,128)S(1)} %dynamic-slice_bitcast_fusion.2, pred[256,2048]{1,0:T(8,128)(4,1)} %fusion.117, bf16[256,12,64]{0,2,1:T(8,128)(2,1)} %bitcast.149, bf16[2048,12,64]{0,2,1:T(8,128)(2,1)} %bitcast.142), kind=kOutput, calls=%fused_computation.18.clone.1 | convolution fusion | flops 836760576 | bytes 54419456 | tf_op jit(solution)/shard_map/while/body/eval_jaxpr/qhe,khe->hqk/dot_general | solution.py:71
  697.9 20.1 %fusion.118 = f32[12,64,256]{2,1,0:T(8,128)} fusion(bf16[2048,12,64]{0,2,1:T(8,128)(2,1)} %bitcast.140, f32[12,256,2048]{2,1,0:T(8,128)} %get-tuple-element.415, f32[12,256,2048]{2,1,0:T(8,128)} %fusion.116, f32[12,256]{1,0:T(8,128)} %get-tuple-element.416, f32[12,256]{1,0:T(8,128)S(1)} %dynamic-slice_bitcast_fusion.2, pred[256,2048]{1,0:T(8,128)(4,1)} %fusion.117), kind=kOutput, calls=%fused_computation.24.clone.1 | convolution fusion | flops 843251712 | bytes 54812672 | tf_op jit(solution)/shard_map/while/body/eval_jaxpr/hqk,khe->qhe/dot_general | solution.py:78
  722.4 15.5 %dynamic_update_slice.24 = f32[4,256,768]{2,0,1:T(4,128)} dynamic-update-slice(f32[4,256,768]{2,0,1:T(4,128)} %get-tuple-element.457, f32[1,256,768]{2,0,1:T(1,128)} %copy.160, s32[]{:T(128)S(6)} %copy.178, s32[]{:T(128)} %constant.66.clone.1..sunk, s32[]{:T(128)} %constant.66.clone.1..sunk) | dynamic-update-slice | bytes 1572868 | tf_op jit(solution)/shard_map/while/body/jit(dynamic_update_index_in_dim)/dynamic_update_slice | solution.py:132
  765.5 19.8 %multiply_reduce_fusion.14 = (f32[12,256]{1,0:T(8,128)}, f32[12,256,2048]{2,1,0:T(8,128)}) fusion(f32[12,256,2048]{2,1,0:T(8,128)} %fusion.116, f32[12,256]{1,0:T(8,128)S(1)} %dynamic-slice_bitcast_fusion.2, pred[256,2048]{1,0:T(8,128)(4,1)} %fusion.117, bf16[256,12,64]{0,2,1:T(8,128)(2,1)} %bitcast.149, bf16[2048,12,64]{0,2,1:T(8,128)(2,1)} %bitcast.142), kind=kOutput, calls=%fused_computation.18.clone.1 | convolution fusion | flops 836760576 | bytes 54419456 | tf_op jit(solution)/shard_map/while/body/eval_jaxpr/qhe,khe->hqk/dot_general | solution.py:71
  785.2 20.1 %fusion.118 = f32[12,64,256]{2,1,0:T(8,128)} fusion(bf16[2048,12,64]{0,2,1:T(8,128)(2,1)} %bitcast.140, f32[12,256,2048]{2,1,0:T(8,128)} %get-tuple-element.415, f32[12,256,2048]{2,1,0:T(8,128)} %fusion.116, f32[12,256]{1,0:T(8,128)} %get-tuple-element.416, f32[12,256]{1,0:T(8,128)S(1)} %dynamic-slice_bitcast_fusion.2, pred[256,2048]{1,0:T(8,128)(4,1)} %fusion.117), kind=kOutput, calls=%fused_computation.24.clone.1 | convolution fusion | flops 843251712 | bytes 54812672 | tf_op jit(solution)/shard_map/while/body/eval_jaxpr/hqk,khe->qhe/dot_general | solution.py:78
  809.7 15.5 %dynamic_update_slice.24 = f32[4,256,768]{2,0,1:T(4,128)} dynamic-update-slice(f32[4,256,768]{2,0,1:T(4,128)} %get-tuple-element.457, f32[1,256,768]{2,0,1:T(1,128)} %copy.160, s32[]{:T(128)S(6)} %copy.178, s32[]{:T(128)} %constant.66.clone.1..sunk, s32[]{:T(128)} %constant.66.clone.1..sunk) | dynamic-update-slice | bytes 1572868 | tf_op jit(solution)/shard_map/while/body/jit(dynamic_update_index_in_dim)/dynamic_update_slice | solution.py:132
  857.3 20.1 %copy.110 = bf16[4,2048,768]{1,2,0:T(8,128)(2,1)} copy(bf16[4,2048,768]{2,0,1:T(4,128)(2,1)} %all-gather.9.cloned.1.call-done) | data formatting | bytes 25165824 | tf_op jit(solution)/shard_map/all_gather | solution.py:183
  877.5 39.7 %fusion.62 = f32[4,12,2048,256]{3,2,1,0:T(8,128)} fusion(bf16[4,2048,12,64]{1,3,2,0:T(8,128)(2,1)} %bitcast.147, bf16[4,256,12,64]{1,3,2,0:T(8,128)(2,1)} %bitcast.153), kind=kOutput, calls=%fused_computation.137 | convolution fusion | flops 3221225472 | bytes 114819072 | tf_op jit(solution)/shard_map/vmap(qhe,khe->hqk)/dot_general | solution.py:41
  917.2 16.0 %copy.112 = bf16[4,2048,768]{1,2,0:T(8,128)(2,1)} copy(bf16[4,2048,768]{2,1,0:T(8,128)(2,1)} %all-gather.11.cloned.1.call-done) | data formatting | bytes 25165824 | tf_op jit(solution)/shard_map/all_gather | solution.py:184
  933.2 38.9 %fusion.13 = f32[4,12,64,256]{3,2,1,0:T(8,128)} fusion(bf16[4,2048,12,64]{1,3,2,0:T(8,128)(2,1)} %bitcast.150, f32[4,12,2048,256]{3,2,1,0:T(8,128)} %fusion.62, f32[4,12,2048]{2,1,0:T(8,128)} %all_gather.21, pred[4,2048,256]{2,1,0:T(8,128)(4,1)} %broadcast_and_fusion), kind=kOutput, calls=%fused_computation.38 | convolution fusion | flops 3321888768 | bytes 118882304 | tf_op jit(solution)/shard_map/vmap(hqk,qhe->khe)/dot_general | solution.py:202
  977.1 51.0 %fusion.42 = f32[4,12,64,256]{3,2,1,0:T(8,128)} fusion(bf16[4,2048,12,64]{1,3,2,0:T(8,128)(2,1)} %bitcast.148, f32[4,12,2048,256]{3,2,1,0:T(8,128)} %fusion.62, f32[4,12,2048]{2,1,0:T(8,128)} %all_gather.23, f32[4,12,2048]{2,1,0:T(8,128)} %all_gather.21, pred[4,2048,256]{2,1,0:T(8,128)(4,1)} %broadcast_and_fusion, bf16[4,2048,12,64]{1,3,2,0:T(8,128)(2,1)} %bitcast.151, ...), kind=kOutput, calls=%fused_computation.94 | convolution fusion | flops 6594232320 | bytes 133431296 | tf_op jit(solution)/shard_map/vmap(hqk,qhe->khe)/dot_general | solution.py:197
  1033.0 20.5 %multiply_reduce_fusion.2 = (f32[2304]{0:T(1024)}, f32[2304]{0:T(1024)}, f32[2304]{0:T(1024)S(1)}, f32[4,256,2304]{2,0,1:T(4,128)S(1)}) fusion(f32[4,258,2304]{2,0,1:T(4,128)} %constant_dynamic-update-slice_fusion.1, f32[4,256,768]{2,0,1:T(4,128)} %copy.116, f32[4,256,768]{2,0,1:T(4,128)} %copy.115, f32[4,256,768]{2,0,1:T(4,128)} %get-tuple-element.108, ...), kind=kLoop, calls=%fused_computation.49 | loop fusion | flops 18867456 | bytes 47213568 | tf_op jit(solution)/shard_map/reduce_sum | solution.py:231
  1082.8 26.9 %all-reduce.4 = (f32[3,2304]{1,0:T(4,128)}, f32[4]{0:T(128)S(1)}) all-reduce(f32[3,2304]{1,0:T(4,128)} %pad_maximum_fusion.2, f32[4]{0:T(128)} %pad_maximum_fusion.3), channel_id=1, replica_groups=mesh['seq'=8,'batch'=4] {'seq'}, use_global_device_ids=true, to_apply=%region_19.20 | all-reduce | flops 6916 | bytes 55328 | tf_op jit(solution)/shard_map/psum | solution.py:271
  1109.7 25.1 %all-reduce.5 = (f32[3,2304]{1,0:T(4,128)}, f32[4]{0:T(128)S(1)}) all-reduce(f32[3,2304]{1,0:T(4,128)} %get-tuple-element.254, f32[4]{0:T(128)S(1)} %get-tuple-element.255), channel_id=1, replica_groups=mesh['seq'=8,'batch'=4] {'batch'}, use_global_device_ids=true, to_apply=%region_20.21 | all-reduce | flops 6916 | bytes 55328 | tf_op jit(solution)/shard_map/psum | solution.py:271
  1168.1 12.6 %all-reduce.6 = (bf16[192]{0:T(256)(128)(2,1)}, bf16[192]{0:T(256)(128)(2,1)}) all-reduce(bf16[192]{0:T(256)(128)(2,1)S(1)} %dynamic-slice.1, bf16[192]{0:T(256)(128)(2,1)} %dynamic-slice.3), channel_id=1, replica_groups=mesh['seq'=8,'batch'=4] {'seq'}, use_global_device_ids=true, to_apply=%region_13.14 | all-reduce | flops 384 | bytes 1536 | tf_op jit(solution)/shard_map/psum | solution.py:262
  1188.8 34.7 %all-reduce.11.cloned.1.call-done = (bf16[192,2304]{1,0:T(8,128)(2,1)}, bf16[192,768]{1,0:T(8,128)(2,1)}, bf16[192,3072]{1,0:T(8,128)(2,1)}, bf16[768,768]{1,0:T(8,128)(2,1)}) async-done(((bf16[192,2304]{1,0:T(8,128)(2,1)}, bf16[192,768]{1,0:T(8,128)(2,1)}, bf16[192,3072]{1,0:T(8,128)(2,1)}, bf16[768,768]{1,0:T(8,128)(2,1)}), (bf16[192,2304]{1,0:T(8,128)(2,1)}, bf16[192,768]{1,0:T(8,128)(2,1)}, ...) | async-done | bytes 3538960 | tf_op jit(solution)/shard_map/psum | solution.py:263
  (260 shorter events, 494.5 us)
Async XLA Ops:
  7.2 127.6 %all-gather.7.cloned.1.call-start = ((), (), s32[]{:S(2)}) async-start(), calls=%async_computation.5 | async-start | bytes 14155776 | tf_op jit(solution)/shard_map/all_gather | solution.py:125
  8.1 8.0 copy-start.23
  10.7 5.4 copy-start.20
  10.7 11.6 copy-start.16
  19.7 3.3 collective-permute-start
  22.9 14.0 %copy-start.10 = (f32[2304]{0:T(1024)}, f32[2304]{0:T(1024)S(1)}, u32[]{:S(2)}) copy-start(f32[2304]{0:T(1024)S(1)} %get-tuple-element.212) | copy-start | bytes 27652
  57.4 151.4 %all-gather.5.cloned.1.call-start = ((), (), s32[]{:S(2)}) async-start(), calls=%async_computation.4 | async-start | bytes 14155776 | tf_op jit(solution)/shard_map/all_gather | solution.py:126
  58.2 799.2 %all-gather.9.cloned.1.call-start = ((), (), s32[]{:S(2)}) async-start(), calls=%async_computation.6 | async-start | bytes 14155776 | tf_op jit(solution)/shard_map/all_gather | solution.py:183
  64.5 852.7 %all-gather.11.cloned.1.call-start = ((), (), s32[]{:S(2)}) async-start(), calls=%async_computation.7 | async-start | bytes 14155776 | tf_op jit(solution)/shard_map/all_gather | solution.py:184
  399.8 13.6 %slice-start = ((s8[4718592]{0:T(1024)(128)(4,1)}), s8[4194304]{0:T(1024)(128)(4,1)S(1)}, s32[]{:S(2)}) async-start(s8[4718592]{0:T(1024)(128)(4,1)} %bitcast.157), calls=%async_computation.13 | async-start | bytes 8388608
  404.9 36.1 %copy-start.6 = (f32[4,256,768]{2,1,0:T(8,128)}, f32[4,256,768]{2,1,0:T(8,128)S(1)}, u32[]{:S(2)}) copy-start(f32[4,256,768]{2,1,0:T(8,128)S(1)} %get-tuple-element.269) | copy-start | bytes 9437188
  404.9 36.1 %copy-start.17 = (f32[4,256]{1,0:T(4,128)}, f32[4,256]{1,0:T(4,128)S(1)}, u32[]{:S(2)}) copy-start(f32[4,256]{1,0:T(4,128)S(1)} %get-tuple-element.289) | copy-start | bytes 12292
  404.9 8.5 copy-start.7
  404.9 8.5 copy-start.14
  404.9 8.5 slice-start.1
  446.4 689.7 %reduce-scatter.7.cloned.1.call-start = ((), (), s32[]{:S(2)}) async-start(), calls=%async_computation.9 | async-start | bytes 1474560 | tf_op jit(solution)/shard_map/reduce_scatter | solution.py:248
  452.5 683.6 %reduce-scatter.11.cloned.1.call-start = ((), (), s32[]{:S(2)}) async-start(), calls=%async_computation.11 | async-start | bytes 5898240 | tf_op jit(solution)/shard_map/reduce_scatter | solution.py:257
  474.1 662.0 %reduce-scatter.9.cloned.1.call-start = ((), (), s32[]{:S(2)}) async-start(), calls=%async_computation.10 | async-start | bytes 5898240 | tf_op jit(solution)/shard_map/reduce_scatter | solution.py:254
  857.3 287.8 %reduce-scatter.5.cloned.1.call-start = ((), (), s32[]{:S(2)}) async-start(), calls=%async_computation.8 | async-start | bytes 4423680 | tf_op jit(solution)/shard_map/reduce_scatter | solution.py:245
  1033.0 20.5 %copy-start.11 = (f32[2304]{0:T(1024)S(1)}, f32[2304]{0:T(1024)}, u32[]{:S(2)}) copy-start(f32[2304]{0:T(1024)} %copy-done.10) | copy-start | bytes 27652
  1033.0 20.5 %copy-start.12 = (f32[2304]{0:T(1024)S(1)}, f32[2304]{0:T(1024)}, u32[]{:S(2)}) copy-start(f32[2304]{0:T(1024)} %get-tuple-element.213) | copy-start | bytes 27652
  1033.0 24.4 %copy-start.13 = (f32[2304]{0:T(1024)S(1)}, f32[2304]{0:T(1024)}, u32[]{:S(2)}) copy-start(f32[2304]{0:T(1024)} %get-tuple-element.211) | copy-start | bytes 27652
  1053.6 15.0 %copy-start.4 = (bf16[4,256,768]{2,1,0:T(8,128)(2,1)S(1)}, bf16[4,256,768]{2,1,0:T(8,128)(2,1)}, u32[]{:S(2)}) copy-start(bf16[4,256,768]{2,1,0:T(8,128)(2,1)} %param.15) | copy-start | bytes 4718596
  1053.6 15.0 %copy-start.21 = (f32[4,256]{1,0:T(4,128)S(1)}, f32[4,256]{1,0:T(4,128)}, u32[]{:S(2)}) copy-start(f32[4,256]{1,0:T(4,128)} %copy-done.20) | copy-start | bytes 12292
  1053.6 15.0 %copy-start.24 = (f32[768]{0:T(1024)S(1)}, f32[768]{0:T(1024)}, u32[]{:S(2)}) copy-start(f32[768]{0:T(1024)} %copy-done.23) | copy-start | bytes 9220
  1053.7 3.8 collective-permute-start.1
  1074.2 149.3 %all-reduce.11.cloned.1.call-start = ((), (), s32[]{:S(2)}) async-start(), calls=%async_computation.12 | async-start | bytes 7077888 | tf_op jit(solution)/shard_map/psum | solution.py:263
  1077.5 68.1 %copy-start.22 = (f32[4,256]{1,0:T(4,128)S(1)}, f32[4,256]{1,0:T(4,128)}, u32[]{:S(2)}) copy-start(f32[4,256]{1,0:T(4,128)} %copy-done.20) | copy-start | bytes 12292
  1082.1 63.5 %copy-start.25 = (f32[768]{0:T(1024)S(1)}, f32[768]{0:T(1024)}, u32[]{:S(2)}) copy-start(f32[768]{0:T(1024)} %copy-done.23) | copy-start | bytes 9220
  1145.6 9.2 copy-start.31
  1145.6 38.3 %copy-start.19 = (f32[4,256]{1,0:T(4,128)S(1)}, f32[4,256]{1,0:T(4,128)}, u32[]{:S(2)}) copy-start(f32[4,256]{1,0:T(4,128)} %get-tuple-element.286) | copy-start | bytes 12292
  1223.5 6.1 copy-start.8
  (18 other events, 54.3 us)
Sparse Core Ops, SparseCore 0:
  57.5 77.2 all-gather.6
  136.7 72.1 all-gather.4
  210.8 72.1 all-gather.8
  446.5 72.1 all-gather.10
  520.9 29.1 reduce-scatter.6
  552.3 83.9 reduce-scatter.10
  857.4 85.4 reduce-scatter.8
  1074.3 70.6 reduce-scatter.4
  1148.7 74.6 all-reduce.10
